TPU v7x, 256 devices: a whole 4x4x8 slice. The times are simulated.
256 devices in a mesh: grp: 16 (over z, y_lo), blk: 16 (over y_hi, x, core).
Axes of the slice: x: 4, y: 4 (y_hi: 2, y_lo: 2; y = y_hi * 2 + y_lo), z: 8, core: 2. Of those that a mesh axis runs over, the one named last changes fastest.
Arguments:
- states: bfloat16 [524288, 768], P(('grp', 'blk')), may hold values from -6 to 6
- query_weight: bfloat16 [768, 768], replicated, may hold values from -0.21875 to 0.21875
- attempts: bfloat16 [16384, 768], P(('grp', 'blk')), may hold values from -6 to 6
- attempt_theorem: int32 [16384], P('grp'), may hold values from 0 to 15
- positive: int32 [524288], P(('grp', 'blk')), may hold values from 0 to 1023
Outputs:
- loss: float32 [524288], P(('grp', 'blk'))
- grad_attempts: float32 [16384, 768], P(('grp', 'blk'))
- grad_weight: float32 [768, 768], replicated
All inputs are finite; a program needn't handle non-finite values.
Results may differ from a plain program's by a relative error of at most 0.012.
Values may be sent and summed in bfloat16 or wider, within the bound.
No kernel may reach another device: no remote copies, remote signals or barrier semaphores. Data moves between devices by JAX's collectives and lax.ppermute only.
A program may use at most 64 MiB of HBM per device.

v0:
```python
import functools
import itertools

import jax
import jax.numpy as jnp
from jax import lax
from jax.experimental import pallas as pl
from jax.experimental.pallas import tpu as pltpu
from jax.sharding import Mesh, PartitionSpec as P


SHARP = 0.07
EPS = 1e-06
LOG2E = 1.4426950408889634
AXES = ("z", "yl", "yh", "x", "c")
SIZES = (8, 2, 2, 4, 2)
PLANE = ("yh", "yl", "x")
ROW = ("yh", "x")
SUB = 256
BF, F32 = jnp.bfloat16, jnp.float32
Q_TILE = 512


def flat(coords):
    index = 0
    for value, size in zip(coords, SIZES):
        index = index * size + value % size
    return index


def send(value, move):
    pairs = [(flat(at), flat(move(*at))) for at in itertools.product(*map(range, SIZES))]
    return lax.ppermute(value, AXES, pairs)


def to_core(value):
    return send(value, lambda z, yl, yh, x, c: (z, yl, yh, x, c ^ 1))


def to_z(value, where):
    return send(value, lambda z, yl, yh, x, c: (where(z), yl, yh, x, c))


def unit_kernel(attempts, spread, scale):
    a = attempts[...].astype(F32)
    r = lax.rsqrt(jnp.sum(a * a, axis=1, keepdims=True) * (1.0 / a.shape[1]) + EPS)
    u = (a * r).astype(BF)
    for k in range(spread.shape[0]):
        spread[k] = u
    scale[...] = r


def unit_rows(attempts):
    rows, width = attempts.shape
    return pl.pallas_call(
        unit_kernel,
        out_shape=[
            jax.ShapeDtypeStruct((8, rows, width), BF),
            jax.ShapeDtypeStruct((rows, 1), F32),
        ],
        cost_estimate=pl.CostEstimate(
            flops=4 * rows * width, bytes_accessed=18 * rows * width, transcendentals=0
        ),
        name="unit",
    )(attempts)


def row_ids(core, half, rows):
    r = lax.broadcasted_iota(jnp.int32, (half, 1), 0)
    return r + (r // rows + core) * rows


def proj_kernel(rows, core, states, weight, labels, positive,
                proj, query, scale, label_q, states_t, weight_t):
    @pl.when(pl.program_id(0) == 0)
    def _():
        weight_t[...] = weight[...].T

    half = labels.shape[0] // 2
    pos = positive[...]
    first = jnp.where(row_ids(core[0], half, rows) == pos, labels[:half, :], 0.0)
    second = jnp.where(row_ids(1 - core[0], half, rows) == pos, labels[half:, :], 0.0)
    label_q[...] = jnp.sum(first + second, axis=0, keepdims=True)
    states_t[...] = states[...].T
    p = jnp.dot(weight_t[...], states_t[...], preferred_element_type=F32)
    r = lax.rsqrt(jnp.sum(p * p, axis=0, keepdims=True) * (1.0 / p.shape[0]) + EPS)
    proj[...] = p
    query[...] = (p * r).astype(BF)
    scale[...] = r


def column(rows):
    return pl.BlockSpec((rows, Q_TILE), lambda i: (0, i))


def whole(shape):
    return pl.BlockSpec(shape, lambda i: (0, 0))


SCALAR = pl.BlockSpec(memory_space=pltpu.SMEM)


def project(core, states, weight, labels, positive, rows):
    queries, width = states.shape
    return pl.pallas_call(
        functools.partial(proj_kernel, rows),
        grid=(queries // Q_TILE,),
        in_specs=[
            SCALAR,
            pl.BlockSpec((Q_TILE, width), lambda i: (i, 0)),
            whole((width, width)), whole(labels.shape), column(1),
        ],
        out_specs=[column(width), column(width), column(1), column(1), column(width)],
        out_shape=[
            jax.ShapeDtypeStruct((width, queries), F32),
            jax.ShapeDtypeStruct((width, queries), BF),
            jax.ShapeDtypeStruct((1, queries), F32),
            jax.ShapeDtypeStruct((1, queries), F32),
            jax.ShapeDtypeStruct((width, queries), BF),
        ],
        scratch_shapes=[pltpu.VMEM((width, width), BF)],
        cost_estimate=pl.CostEstimate(
            flops=2 * queries * width * width,
            bytes_accessed=queries * width * 10,
            transcendentals=0,
        ),
        name="project",
    )(core, states, weight, labels, positive)


def loss_kernel(mult, rows, core, proj, query, scale, label_q, states_t, own, other,
                labels, positive, loss, weights, keep, give, own_t, other_t, total_w):
    step = pl.program_id(0)

    @pl.when(step == 0)
    def _():
        own_t[...] = own[...].T
        other_t[...] = other[...].T
        total_w[...] = jnp.zeros_like(total_w)

    half = own.shape[0]
    width = own.shape[1]
    label_a, label_b = labels[:half, :], labels[half:, :]
    ids_a = row_ids(core[0], half, rows)
    ids_b = row_ids(1 - core[0], half, rows)
    parts = []
    for k in range(Q_TILE // SUB):
        cols = slice(k * SUB, (k + 1) * SUB)
        q = query[:, cols]
        s_a = jnp.dot(own[...], q, preferred_element_type=F32)
        s_b = jnp.dot(other[...], q, preferred_element_type=F32)
        parts.append((cols, s_a, s_b))
    for cols, s_a, s_b in parts:
        pos = positive[:, cols]
        wanted = label_q[:, cols]
        chosen_a = ids_a == pos
        chosen_b = ids_b == pos
        pick = jnp.sum(jnp.where(chosen_a, s_a, 0.0), axis=0, keepdims=True)
        pick += jnp.sum(jnp.where(chosen_b, s_b, 0.0), axis=0, keepdims=True)
        e_a = jnp.where(label_a == wanted, jnp.exp2(s_a * (mult * LOG2E)), 0.0)
        e_b = jnp.where(label_b == wanted, jnp.exp2(s_b * (mult * LOG2E)), 0.0)
        total = jnp.sum(e_a, axis=0, keepdims=True) + jnp.sum(e_b, axis=0, keepdims=True)
        loss[:, cols] = jnp.log(total) - pick * mult
        inv = 1.0 / total
        w_a = (e_a * inv - jnp.where(chosen_a, 1.0, 0.0)).astype(BF)
        w_b = (e_b * inv - jnp.where(chosen_b, 1.0, 0.0)).astype(BF)
        weights[:half, cols] = w_a
        weights[half:, cols] = w_b
        g = jnp.dot(own_t[...], w_a, preferred_element_type=F32)
        g += jnp.dot(other_t[...], w_b, preferred_element_type=F32)
        r = scale[:, cols]
        u = proj[:, cols] * r
        inner = jnp.sum(u * g, axis=0, keepdims=True) * (1.0 / width)
        grad_proj = ((g - u * inner) * (r * mult)).astype(BF)
        total_w[...] += lax.dot_general(
            states_t[:, cols], grad_proj, (((1,), (1,)), ((), ())), preferred_element_type=F32
        )

    @pl.when(step == pl.num_programs(0) - 1)
    def _():
        half_w = width // 2
        keep[...] = total_w[pl.ds(pl.multiple_of(core[0] * half_w, half_w), half_w), :]
        rest = total_w[pl.ds(pl.multiple_of((1 - core[0]) * half_w, half_w), half_w), :]
        give[...] = rest.astype(BF)


def losses_and_weights(mult, core, proj, query, scale, label_q, states_t, own, other,
                       labels, positive, rows):
    width, queries = proj.shape
    half = own.shape[0]
    half_w = width // 2
    return pl.pallas_call(
        functools.partial(loss_kernel, mult, rows),
        grid=(queries // Q_TILE,),
        in_specs=[
            SCALAR, column(width), column(width), column(1), column(1), column(width),
            whole(own.shape), whole(other.shape), whole(labels.shape), column(1),
        ],
        out_specs=[column(1), column(2 * half), whole((half_w, width)), whole((half_w, width))],
        out_shape=[
            jax.ShapeDtypeStruct((1, queries), F32),
            jax.ShapeDtypeStruct((2 * half, queries), BF),
            jax.ShapeDtypeStruct((half_w, width), F32),
            jax.ShapeDtypeStruct((half_w, width), BF),
        ],
        scratch_shapes=[
            pltpu.VMEM((width, half), BF),
            pltpu.VMEM((width, half), BF),
            pltpu.VMEM((width, width), F32),
        ],
        cost_estimate=pl.CostEstimate(
            flops=8 * queries * width * half + 2 * queries * width * width,
            bytes_accessed=queries * width * 12,
            transcendentals=2 * half * queries,
        ),
        name="losses",
    )(core, proj, query, scale, label_q, states_t, own, other, labels, positive)


def on_device(states, query_weight, attempts, attempt_theorem, positive):
    width = states.shape[1]
    mult = 1.0 / (SHARP * width)
    rows = attempts.shape[0]
    c = lax.axis_index("c")
    core = c.reshape(1)

    spread_a, a_scale = unit_rows(attempts)
    own = lax.all_to_all(spread_a, ROW, 0, 0).reshape(-1, width)
    other = to_core(own)

    by_core = attempt_theorem.astype(F32).reshape(8, 2, rows)
    even, odd = by_core[:, 0].reshape(-1), by_core[:, 1].reshape(-1)
    labels = jnp.concatenate([jnp.where(c == 0, even, odd), jnp.where(c == 0, odd, even)])
    labels = labels.reshape(-1, 1)
    pos = positive.reshape(1, -1)

    proj, query, scale, label_q, states_t = project(core, states, query_weight, labels, pos, rows)
    loss, weights, w_keep, w_give = losses_and_weights(
        mult, core, proj, query, scale, label_q, states_t, own, other, labels, pos, rows
    )

    half_a = own.shape[0]
    contract = (((1,), (1,)), ((), ()))
    w_sum = (w_keep + to_core(w_give).astype(F32)).astype(BF)
    parts = lax.all_to_all(w_sum.reshape(16, -1, width), PLANE, 0, 0)
    a_give = lax.dot_general(
        weights[half_a:], query, contract, preferred_element_type=F32
    ).astype(BF)
    a_keep = lax.dot_general(weights[:half_a], query, contract, preferred_element_type=F32)
    a_sum = (a_keep + to_core(a_give).astype(F32)).astype(BF)

    piece = jnp.sum(parts.astype(F32), axis=0).astype(BF)
    a_parts = lax.all_to_all(a_sum.reshape(8, rows, width), ROW, 0, 0)
    moved = to_z(piece, lambda z: z ^ 1)
    piece = (piece.astype(F32) + moved.astype(F32)).astype(BF)
    far, up, down = (to_z(piece, lambda z, s=s: z + s) for s in (4, 2, 6))
    even = piece.astype(F32) + far.astype(F32)
    odd = up.astype(F32) + down.astype(F32)
    piece = (even + odd).astype(BF)
    a_unit = attempts.astype(F32) * a_scale
    g = jnp.sum(a_parts.astype(F32), axis=0)
    inner = jnp.mean(a_unit * g, axis=-1, keepdims=True)
    grad_attempts = (g - a_unit * inner) * (a_scale * mult)

    spread = jnp.broadcast_to(piece[None], (16,) + piece.shape)
    w_half = lax.all_to_all(spread, PLANE, 0, 0).reshape(-1, width)
    w_rest = to_core(w_half)
    low = jnp.where(c == 0, w_half, w_rest)
    high = jnp.where(c == 0, w_rest, w_half)
    grad_weight = jnp.concatenate([low, high], axis=0).astype(F32)
    return (loss.reshape(-1), grad_attempts, grad_weight)


def solution(mesh):
    fine = Mesh(mesh.devices.reshape(SIZES), AXES)
    slices, everyone = P(("z", "yl")), P(AXES)

    return jax.shard_map(
        on_device,
        mesh=fine,
        in_specs=(everyone, P(), everyone, slices, everyone),
        out_specs=(everyone, everyone, P()),
        check_vma=False,
    )
```

profile of v0, /device:TPU:2, one launch (start us, length us, event | category | flops | bytes accessed | tf_op | source)
XLA Modules:
  0.0 127.3 jit_solution(14005221990560044528)
XLA Ops:
  0.6 1.9 %unit.1 = (bf16[8,64,768]{2,1,0:T(8,128)(2,1)}, f32[64,1]{1,0:T(8,128)}) custom-call(bf16[64,768]{1,0:T(8,128)(2,1)} %attempts.1), custom_call_target="tpu_custom_call" | custom-call | flops 196608 | bytes 884736 | tf_op jit(solution)/shard_map/unit/pallas_call | solution.py:55
  2.6 20.7 %all_to_all.20 = bf16[8,64,768]{2,1,0:T(8,128)(2,1)S(1)} all-to-all(bf16[8,64,768]{2,1,0:T(8,128)(2,1)} %get-tuple-element.19), channel_id=1, replica_groups=mesh['z'=8,'yl'=2,'yh'=2,'x'=4,'c'=2] {'yh','x'}, dimensions={0} | all-to-all | bytes 1572864 | tf_op jit(solution)/shard_map/all_to_all | solution.py:228
  23.3 0.7 convert_element_type.53
  24.3 1.0 copy.8.labels
  25.3 9.2 %project.1 = (f32[768,2048]{1,0:T(8,128)}, bf16[768,2048]{1,0:T(8,128)(2,1)}, f32[1,2048]{1,0:T(1,128)}, f32[1,2048]{1,0:T(1,128)}, bf16[768,2048]{1,0:T(8,128)(2,1)}) custom-call(s32[1]{0:T(128)} %bitcast.core, bf16[2048,768]{1,0:T(8,128)(2,1)} %states.1, bf16[768,768]{1,0:T(8,128)(2,1)} %weight.1, f32[1024,1]{1,0:T(8,128)} %copy.8.labels, s32[1,2048]{1,0:T(1,128)} %bitcast.16), custom_call_target="tpu_custom_call" | custom-call | flops 2415919104 | bytes 15728640 | tf_op jit(solution)/shard_map/project/pallas_call | solution.py:105
  34.5 0.9 copy-done.3
  35.4 19.3 %losses.1 = (f32[1,2048]{1,0:T(1,128)}, bf16[1024,2048]{1,0:T(8,128)(2,1)}, f32[384,768]{1,0:T(8,128)}, bf16[384,768]{1,0:T(8,128)(2,1)}) custom-call(s32[1]{0:T(128)} %bitcast.core, f32[768,2048]{1,0:T(8,128)} %get-tuple-element.14.proj, bf16[768,2048]{1,0:T(8,128)(2,1)} %get-tuple-element.15.query, f32[1,2048]{1,0:T(1,128)} %get-tuple-element.16.scale, ...), custom_call_target="tpu_custom_call" | custom-call | flops 8858370048 | bytes 18874368 | tf_op jit(solution)/shard_map/losses/pallas_call | solution.py:192
  54.7 0.6 collective-permute-start.2
  55.3 1.8 %collective-permute-done.2 = bf16[384,768]{1,0:T(8,128)(2,1)S(1)} collective-permute-done((bf16[384,768]{1,0:T(8,128)(2,1)}, bf16[384,768]{1,0:T(8,128)(2,1)S(1)}, u32[]{:S(2)}, u32[]{:S(2)}) %collective-permute-start.2) | collective-permute-done | bytes 589856 | tf_op jit(solution)/shard_map/ppermute | solution.py:33
  57.1 2.2 %add_convert_fusion.1 = bf16[384,768]{1,0:T(8,128)(2,1)} fusion(f32[384,768]{1,0:T(8,128)} %get-tuple-element.23, bf16[384,768]{1,0:T(8,128)(2,1)S(1)} %collective-permute-done.2), kind=kLoop, calls=%fused_computation.8 | loop fusion | flops 884736 | bytes 2359296 | tf_op jit(solution)/shard_map/convert_element_type | solution.py:244
  59.3 4.5 %all-to-all-start.2 = ((bf16[16,24,768]{2,1,0:T(8,128)(2,1)}), bf16[16,24,768]{2,1,0:T(8,128)(2,1)S(1)}, u32[]{:S(2)}, u32[]{:S(2)}) async-start(bf16[16,24,768]{2,1,0:T(8,128)(2,1)} %bitcast.6), calls=%async_computation.2 | async-start | bytes 1179648 | tf_op jit(solution)/shard_map/all_to_all | solution.py:245
  63.8 4.3 %fusion.6 = bf16[512,768]{1,0:T(8,128)(2,1)S(1)} fusion(bf16[768,2048]{1,0:T(8,128)(2,1)} %get-tuple-element.15.query, bf16[1024,2048]{1,0:T(8,128)(2,1)} %get-tuple-element.21), kind=kOutput, calls=%fused_computation.6 | convolution fusion | flops 1611005952 | bytes 6029312 | tf_op jit(solution)/shard_map/dot_general | solution.py:246
  68.2 0.2 collective-permute-start.1
  68.4 7.2 %all-to-all-done.2 = bf16[16,24,768]{2,1,0:T(8,128)(2,1)S(1)} async-done(((bf16[16,24,768]{2,1,0:T(8,128)(2,1)}), bf16[16,24,768]{2,1,0:T(8,128)(2,1)S(1)}, u32[]{:S(2)}, u32[]{:S(2)}) %all-to-all-start.2) | async-done | bytes 589856 | tf_op jit(solution)/shard_map/all_to_all | solution.py:245
  75.7 2.0 %collective-permute-start.3 = (bf16[24,768]{1,0:T(8,128)(2,1)S(1)}, bf16[24,768]{1,0:T(8,128)(2,1)S(1)}, u32[]{:S(2)}, u32[]{:S(2)}) collective-permute-start(bf16[24,768]{1,0:T(8,128)(2,1)S(1)} %reduce_sum.32), channel_id=1, source_target_pairs={{0,32},{1,33},{2,34},{3,35},{4,36},{5,37},{6,38},{7,39},{8,40},{9,... | collective-permute-start | bytes 110600 | tf_op jit(solution)/shard_map/ppermute | solution.py:33
  77.7 2.0 %collective-permute-done.3 = bf16[24,768]{1,0:T(8,128)(2,1)S(1)} collective-permute-done((bf16[24,768]{1,0:T(8,128)(2,1)S(1)}, bf16[24,768]{1,0:T(8,128)(2,1)S(1)}, u32[]{:S(2)}, u32[]{:S(2)}) %collective-permute-start.3) | collective-permute-done | bytes 36896 | tf_op jit(solution)/shard_map/ppermute | solution.py:33
  79.8 6.4 %collective-permute-start.6 = (bf16[24,768]{1,0:T(8,128)(2,1)S(1)}, bf16[24,768]{1,0:T(8,128)(2,1)S(1)}, u32[]{:S(2)}, u32[]{:S(2)}) collective-permute-start(bf16[24,768]{1,0:T(8,128)(2,1)S(1)} %add_convert_fusion.3), channel_id=1, source_target_pairs={{0,192},{1,193},{2,194},{3,195},{4,196},{5,197},{6,198},{7,199},{8... | collective-permute-start | bytes 110600 | tf_op jit(solution)/shard_map/ppermute | solution.py:33
  86.1 3.8 %collective-permute-start.4 = (bf16[24,768]{1,0:T(8,128)(2,1)S(1)}, bf16[24,768]{1,0:T(8,128)(2,1)S(1)}, u32[]{:S(2)}, u32[]{:S(2)}) collective-permute-start(bf16[24,768]{1,0:T(8,128)(2,1)S(1)} %add_convert_fusion.3), channel_id=1, source_target_pairs={{0,128},{1,129},{2,130},{3,131},{4,132},{5,133},{6,134},{7,135},{8... | collective-permute-start | bytes 110600 | tf_op jit(solution)/shard_map/ppermute | solution.py:33
  90.0 2.2 %collective-permute-done.5 = bf16[24,768]{1,0:T(8,128)(2,1)S(1)} collective-permute-done((bf16[24,768]{1,0:T(8,128)(2,1)S(1)}, bf16[24,768]{1,0:T(8,128)(2,1)S(1)}, u32[]{:S(2)}, u32[]{:S(2)}) %collective-permute-start.5) | collective-permute-done | bytes 36896 | tf_op jit(solution)/shard_map/ppermute | solution.py:33
  92.2 2.0 %collective-permute-done.4 = bf16[24,768]{1,0:T(8,128)(2,1)S(1)} collective-permute-done((bf16[24,768]{1,0:T(8,128)(2,1)S(1)}, bf16[24,768]{1,0:T(8,128)(2,1)S(1)}, u32[]{:S(2)}, u32[]{:S(2)}) %collective-permute-start.4) | collective-permute-done | bytes 36896 | tf_op jit(solution)/shard_map/ppermute | solution.py:33
  94.3 0.9 broadcast_in_dim.2
  95.1 4.8 %all-to-all-start.3 = ((bf16[16,24,768]{2,1,0:T(8,128)(2,1)}), bf16[16,24,768]{2,1,0:T(8,128)(2,1)S(1)}, u32[]{:S(2)}, u32[]{:S(2)}) async-start(bf16[16,24,768]{2,1,0:T(8,128)(2,1)} %broadcast_in_dim.2), calls=%async_computation.3 | async-start | bytes 1179648 | tf_op jit(solution)/shard_map/all_to_all | solution.py:266
  100.0 5.2 %add_convert_fusion = bf16[512,768]{1,0:T(8,128)(2,1)} fusion(bf16[512,768]{1,0:T(8,128)(2,1)S(1)} %collective-permute-done.1, bf16[768,2048]{1,0:T(8,128)(2,1)} %get-tuple-element.15.query, bf16[1024,2048]{1,0:T(8,128)(2,1)} %get-tuple-element.21), kind=kOutput, calls=%fused_computation.5 | convolution fusion | flops 1611792384 | bytes 6815744 | tf_op jit(solution)/shard_map/dot_general | solution.py:249
  105.2 4.0 %all-to-all-done.3 = bf16[16,24,768]{2,1,0:T(8,128)(2,1)S(1)} async-done(((bf16[16,24,768]{2,1,0:T(8,128)(2,1)}), bf16[16,24,768]{2,1,0:T(8,128)(2,1)S(1)}, u32[]{:S(2)}, u32[]{:S(2)}) %all-to-all-start.3) | async-done | bytes 589856 | tf_op jit(solution)/shard_map/all_to_all | solution.py:266
  109.2 4.9 %all-to-all-start.1 = ((bf16[8,64,768]{2,1,0:T(8,128)(2,1)}), bf16[8,64,768]{2,1,0:T(8,128)(2,1)S(1)}, u32[]{:S(2)}, u32[]{:S(2)}) async-start(bf16[8,64,768]{2,1,0:T(8,128)(2,1)} %bitcast.5), calls=%async_computation.1 | async-start | bytes 1572864 | tf_op jit(solution)/shard_map/all_to_all | solution.py:253
  114.1 0.1 fusion.11
  114.3 10.3 %all-to-all-done.1 = bf16[8,64,768]{2,1,0:T(8,128)(2,1)S(1)} async-done(((bf16[8,64,768]{2,1,0:T(8,128)(2,1)}), bf16[8,64,768]{2,1,0:T(8,128)(2,1)S(1)}, u32[]{:S(2)}, u32[]{:S(2)}) %all-to-all-start.1) | async-done | bytes 786464 | tf_op jit(solution)/shard_map/all_to_all | solution.py:253
  124.5 0.1 convert_reduce_fusion
  124.7 0.2 multiply_reduce_fusion
  124.8 0.8 subtract_multiply_fusion
  125.6 0.1 broadcast_select_fusion.1
  125.8 1.6 %maximum_convert_fusion = f32[768,768]{1,0:T(8,128)} fusion(bf16[384,768]{1,0:T(8,128)(2,1)S(1)} %get-tuple-element.30, bf16[384,768]{1,0:T(8,128)(2,1)S(1)} %get-tuple-element.29), kind=kLoop, calls=%fused_computation.7 | loop fusion | flops 2359296 | bytes 3538944 | tf_op jit(solution)/shard_map/convert_element_type | solution.py:270
  (23 shorter events, 0.5 us)
Async XLA Ops:
  23.3 11.2 %copy-start.1 = (bf16[8,64,768]{2,1,0:T(8,128)(2,1)}, bf16[8,64,768]{2,1,0:T(8,128)(2,1)S(1)}, u32[]{:S(2)}) copy-start(bf16[8,64,768]{2,1,0:T(8,128)(2,1)S(1)} %all_to_all.20) | copy-start | bytes 2359300
  23.3 11.2 %collective-permute-start = (bf16[512,768]{1,0:T(8,128)(2,1)S(1)}, bf16[512,768]{1,0:T(8,128)(2,1)S(1)}, u32[]{:S(2)}, u32[]{:S(2)}) collective-permute-start(bf16[512,768]{1,0:T(8,128)(2,1)S(1)} %bitcast.13), channel_id=1, source_target_pairs={{0,1},{1,0},{2,3},{3,2},{4,5},{5,4},{6,7},{7,6},{8,9},{9,8},{10,11... | collective-permute-start | bytes 2359304 | tf_op jit(solution)/shard_map/ppermute | solution.py:33
  34.5 0.9 copy-start.3
  54.7 2.4 %collective-permute-start.2 = (bf16[384,768]{1,0:T(8,128)(2,1)}, bf16[384,768]{1,0:T(8,128)(2,1)S(1)}, u32[]{:S(2)}, u32[]{:S(2)}) collective-permute-start(bf16[384,768]{1,0:T(8,128)(2,1)} %get-tuple-element.24), channel_id=1, source_target_pairs={{0,1},{1,0},{2,3},{3,2},{4,5},{5,4},{6,7},{7,6},{8,9},{9,8},{10,11... | collective-permute-start | bytes 1769480 | tf_op jit(solution)/shard_map/ppermute | solution.py:33
  59.3 16.3 %all-to-all-start.2 = ((bf16[16,24,768]{2,1,0:T(8,128)(2,1)}), bf16[16,24,768]{2,1,0:T(8,128)(2,1)S(1)}, u32[]{:S(2)}, u32[]{:S(2)}) async-start(bf16[16,24,768]{2,1,0:T(8,128)(2,1)} %bitcast.6), calls=%async_computation.2 | async-start | bytes 1179648 | tf_op jit(solution)/shard_map/all_to_all | solution.py:245
  68.2 31.8 %collective-permute-start.1 = (bf16[512,768]{1,0:T(8,128)(2,1)S(1)}, bf16[512,768]{1,0:T(8,128)(2,1)S(1)}, u32[]{:S(2)}, u32[]{:S(2)}) collective-permute-start(bf16[512,768]{1,0:T(8,128)(2,1)S(1)} %fusion.6), channel_id=1, source_target_pairs={{0,1},{1,0},{2,3},{3,2},{4,5},{5,4},{6,7},{7,6},{8,9},{9,8},{10,11... | collective-permute-start | bytes 2359304 | tf_op jit(solution)/shard_map/ppermute | solution.py:33
  75.7 4.0 %collective-permute-start.3 = (bf16[24,768]{1,0:T(8,128)(2,1)S(1)}, bf16[24,768]{1,0:T(8,128)(2,1)S(1)}, u32[]{:S(2)}, u32[]{:S(2)}) collective-permute-start(bf16[24,768]{1,0:T(8,128)(2,1)S(1)} %reduce_sum.32), channel_id=1, source_target_pairs={{0,32},{1,33},{2,34},{3,35},{4,36},{5,37},{6,38},{7,39},{8,40},{9,... | collective-permute-start | bytes 110600 | tf_op jit(solution)/shard_map/ppermute | solution.py:33
  79.8 10.2 %collective-permute-start.6 = (bf16[24,768]{1,0:T(8,128)(2,1)S(1)}, bf16[24,768]{1,0:T(8,128)(2,1)S(1)}, u32[]{:S(2)}, u32[]{:S(2)}) collective-permute-start(bf16[24,768]{1,0:T(8,128)(2,1)S(1)} %add_convert_fusion.3), channel_id=1, source_target_pairs={{0,192},{1,193},{2,194},{3,195},{4,196},{5,197},{6,198},{7,199},{8... | collective-permute-start | bytes 110600 | tf_op jit(solution)/shard_map/ppermute | solution.py:33
  86.1 6.1 %collective-permute-start.5 = (bf16[24,768]{1,0:T(8,128)(2,1)S(1)}, bf16[24,768]{1,0:T(8,128)(2,1)S(1)}, u32[]{:S(2)}, u32[]{:S(2)}) collective-permute-start(bf16[24,768]{1,0:T(8,128)(2,1)S(1)} %add_convert_fusion.3), channel_id=1, source_target_pairs={{0,64},{1,65},{2,66},{3,67},{4,68},{5,69},{6,70},{7,71},{8,72},{9,... | collective-permute-start | bytes 110600 | tf_op jit(solution)/shard_map/ppermute | solution.py:33
  86.1 8.1 %collective-permute-start.4 = (bf16[24,768]{1,0:T(8,128)(2,1)S(1)}, bf16[24,768]{1,0:T(8,128)(2,1)S(1)}, u32[]{:S(2)}, u32[]{:S(2)}) collective-permute-start(bf16[24,768]{1,0:T(8,128)(2,1)S(1)} %add_convert_fusion.3), channel_id=1, source_target_pairs={{0,128},{1,129},{2,130},{3,131},{4,132},{5,133},{6,134},{7,135},{8... | collective-permute-start | bytes 110600 | tf_op jit(solution)/shard_map/ppermute | solution.py:33
  95.1 14.0 %all-to-all-start.3 = ((bf16[16,24,768]{2,1,0:T(8,128)(2,1)}), bf16[16,24,768]{2,1,0:T(8,128)(2,1)S(1)}, u32[]{:S(2)}, u32[]{:S(2)}) async-start(bf16[16,24,768]{2,1,0:T(8,128)(2,1)} %broadcast_in_dim.2), calls=%async_computation.3 | async-start | bytes 1179648 | tf_op jit(solution)/shard_map/all_to_all | solution.py:266
  99.9 14.1 %copy-start.2 = (f32[64,1]{1,0:T(8,128)S(1)}, f32[64,1]{1,0:T(8,128)}, u32[]{:S(2)}) copy-start(f32[64,1]{1,0:T(8,128)} %get-tuple-element.22) | copy-start | bytes 772
  105.2 19.5 %copy-start = (bf16[64,768]{1,0:T(8,128)(2,1)S(1)}, bf16[64,768]{1,0:T(8,128)(2,1)}, u32[]{:S(2)}) copy-start(bf16[64,768]{1,0:T(8,128)(2,1)} %attempts.1) | copy-start | bytes 294916
  109.2 15.4 %all-to-all-start.1 = ((bf16[8,64,768]{2,1,0:T(8,128)(2,1)}), bf16[8,64,768]{2,1,0:T(8,128)(2,1)S(1)}, u32[]{:S(2)}, u32[]{:S(2)}) async-start(bf16[8,64,768]{2,1,0:T(8,128)(2,1)} %bitcast.5), calls=%async_computation.1 | async-start | bytes 1572864 | tf_op jit(solution)/shard_map/all_to_all | solution.py:253
  114.2 11.5 %collective-permute-start.7 = (bf16[384,768]{1,0:T(8,128)(2,1)S(1)}, bf16[384,768]{1,0:T(8,128)(2,1)S(1)}, u32[]{:S(2)}, u32[]{:S(2)}) collective-permute-start(bf16[384,768]{1,0:T(8,128)(2,1)S(1)} %bitcast.12), channel_id=1, source_target_pairs={{0,1},{1,0},{2,3},{3,2},{4,5},{5,4},{6,7},{7,6},{8,9},{9,8},{10,11... | collective-permute-start | bytes 1769480 | tf_op jit(solution)/shard_map/ppermute | solution.py:33
where the time goes:
time: 128 us; the launch traced here: 127 us
  Pallas kernels  30.4 us (24%)
  waiting for transfers between devices  29.6 us (23%)
  starting transfers between devices  27.3 us (21%)
  blocking collectives  20.7 us (16%)
  matrix products  9.57 us (7%)
  other arithmetic  5.92 us (5%)
  local copies, waits for them, and re-layouts  3.01 us (2%)
    all_to_all x1, blocking collectives, on_device(): own = lax.all_to_all(spread_a, ROW, 0, 0).reshape(-1, width)  20.7 us
    pallas_call x1, Pallas kernels, losses_and_weights(): pl.pallas_call(functools.partial(loss_kernel, mult, rows), grid=(queries...  19.3 us
    ppermute x8, starting transfers between devices, send(): return lax.ppermute(value, AXES, pairs)  13.1 us
    all_to_all x1, waiting for transfers between devices, on_device(): a_parts = lax.all_to_all(a_sum.reshape(8, rows, width), ROW, 0, 0)  10.3 us
    pallas_call x1, Pallas kernels, project(): pl.pallas_call(functools.partial(proj_kernel, rows), grid=(queries // Q_T...  9.2 us
    ppermute x8, waiting for transfers between devices, send(): return lax.ppermute(value, AXES, pairs)  8.17 us
    all_to_all x1, waiting for transfers between devices, on_device(): parts = lax.all_to_all(w_sum.reshape(16, -1, width), PLANE, 0, 0)  7.25 us
    dot_general x1, matrix products, on_device(): lax.dot_general(weights[:half_a], query, contract, preferred_element_type...  5.23 us
  transfers between devices with their start and end apart: 11, of which 7 were waited for; matrix products, arithmetic and copies ran while one was open for 11% of the time, Pallas kernels for 7%

commit v1 on v0

--- a/solution.py
+++ b/solution.py
@@ -16,9 +16,9 @@
 SIZES = (8, 2, 2, 4, 2)
 PLANE = ("yh", "yl", "x")
 ROW = ("yh", "x")
-SUB = 256
 BF, F32 = jnp.bfloat16, jnp.float32
 Q_TILE = 512
+TILE = 1024
 
 
 def flat(coords):
@@ -71,7 +71,7 @@
 
 
 def proj_kernel(rows, core, states, weight, labels, positive,
-                proj, query, scale, label_q, states_t, weight_t):
+                query, scale, label_q, states_t, weight_t):
     @pl.when(pl.program_id(0) == 0)
     def _():
         weight_t[...] = weight[...].T
@@ -84,7 +84,6 @@
     states_t[...] = states[...].T
     p = jnp.dot(weight_t[...], states_t[...], preferred_element_type=F32)
     r = lax.rsqrt(jnp.sum(p * p, axis=0, keepdims=True) * (1.0 / p.shape[0]) + EPS)
-    proj[...] = p
     query[...] = (p * r).astype(BF)
     scale[...] = r
 
@@ -110,9 +109,8 @@
             pl.BlockSpec((Q_TILE, width), lambda i: (i, 0)),
             whole((width, width)), whole(labels.shape), column(1),
         ],
-        out_specs=[column(width), column(width), column(1), column(1), column(width)],
+        out_specs=[column(width), column(1), column(1), column(width)],
         out_shape=[
-            jax.ShapeDtypeStruct((width, queries), F32),
             jax.ShapeDtypeStruct((width, queries), BF),
             jax.ShapeDtypeStruct((1, queries), F32),
             jax.ShapeDtypeStruct((1, queries), F32),
@@ -121,100 +119,130 @@
         scratch_shapes=[pltpu.VMEM((width, width), BF)],
         cost_estimate=pl.CostEstimate(
             flops=2 * queries * width * width,
-            bytes_accessed=queries * width * 10,
+            bytes_accessed=queries * width * 6,
             transcendentals=0,
         ),
         name="project",
     )(core, states, weight, labels, positive)
 
 
-def loss_kernel(mult, rows, core, proj, query, scale, label_q, states_t, own, other,
-                labels, positive, loss, weights, keep, give, own_t, other_t, total_w):
-    step = pl.program_id(0)
-
-    @pl.when(step == 0)
-    def _():
-        own_t[...] = own[...].T
-        other_t[...] = other[...].T
-        total_w[...] = jnp.zeros_like(total_w)
-
-    half = own.shape[0]
-    width = own.shape[1]
-    label_a, label_b = labels[:half, :], labels[half:, :]
-    ids_a = row_ids(core[0], half, rows)
-    ids_b = row_ids(1 - core[0], half, rows)
-    parts = []
-    for k in range(Q_TILE // SUB):
-        cols = slice(k * SUB, (k + 1) * SUB)
-        q = query[:, cols]
-        s_a = jnp.dot(own[...], q, preferred_element_type=F32)
-        s_b = jnp.dot(other[...], q, preferred_element_type=F32)
-        parts.append((cols, s_a, s_b))
-    for cols, s_a, s_b in parts:
-        pos = positive[:, cols]
-        wanted = label_q[:, cols]
-        chosen_a = ids_a == pos
-        chosen_b = ids_b == pos
-        pick = jnp.sum(jnp.where(chosen_a, s_a, 0.0), axis=0, keepdims=True)
-        pick += jnp.sum(jnp.where(chosen_b, s_b, 0.0), axis=0, keepdims=True)
-        e_a = jnp.where(label_a == wanted, jnp.exp2(s_a * (mult * LOG2E)), 0.0)
-        e_b = jnp.where(label_b == wanted, jnp.exp2(s_b * (mult * LOG2E)), 0.0)
-        total = jnp.sum(e_a, axis=0, keepdims=True) + jnp.sum(e_b, axis=0, keepdims=True)
-        loss[:, cols] = jnp.log(total) - pick * mult
-        inv = 1.0 / total
-        w_a = (e_a * inv - jnp.where(chosen_a, 1.0, 0.0)).astype(BF)
-        w_b = (e_b * inv - jnp.where(chosen_b, 1.0, 0.0)).astype(BF)
-        weights[:half, cols] = w_a
-        weights[half:, cols] = w_b
-        g = jnp.dot(own_t[...], w_a, preferred_element_type=F32)
-        g += jnp.dot(other_t[...], w_b, preferred_element_type=F32)
-        r = scale[:, cols]
-        u = proj[:, cols] * r
+def loss_kernel(mult, rows, tile, core, query_hbm, states_hbm, own_hbm, other_hbm, scale, label_q, labels,
+                 positive, loss, weights_hbm, keep, give,
+                 panel, panel_t, query, states, weights, grad_p, acc_keep, acc_give, sems):
+    half, width = own_hbm.shape
+    queries = query_hbm.shape[1]
+    count = queries // tile
+    cols = [slice(k * tile, (k + 1) * tile) for k in range(count)]
+    panel_in = [
+        pltpu.make_async_copy(own_hbm, panel.at[:half, :], sems.at[0]),
+        pltpu.make_async_copy(other_hbm, panel.at[half:, :], sems.at[1]),
+    ]
+    query_in = [
+        pltpu.make_async_copy(query_hbm.at[:, c], query.at[:, c], sems.at[2 + k])
+        for k, c in enumerate(cols)
+    ]
+    states_in = pltpu.make_async_copy(states_hbm, states, sems.at[2 + count])
+    weights_out = [
+        pltpu.make_async_copy(weights.at[:, c], weights_hbm.at[:, c], sems.at[3 + count + k])
+        for k, c in enumerate(cols)
+    ]
+    for copy in panel_in + query_in + [states_in]:
+        copy.start()
+    ids = jnp.concatenate([row_ids(core[0], half, rows), row_ids(1 - core[0], half, rows)], axis=0)
+    label_j = labels[...]
+    half_w = width // 2
+    mine = pl.ds(pl.multiple_of(core[0] * half_w, half_w), half_w)
+    theirs = pl.ds(pl.multiple_of((1 - core[0]) * half_w, half_w), half_w)
+
+    def scores(k):
+        return jnp.dot(panel[...], query[:, cols[k]], preferred_element_type=F32)
+
+    def soften(k, s):
+        c = cols[k]
+        chosen = ids == positive[:, c]
+        pick = jnp.sum(jnp.where(chosen, s, 0.0), axis=0, keepdims=True)
+        e = jnp.where(label_j == label_q[:, c], jnp.exp2(s * (mult * LOG2E)), 0.0)
+        total = jnp.sum(e, axis=0, keepdims=True)
+        loss[:, c] = jnp.log(total) - pick * mult
+        w = e * (1.0 / total)
+        weights[:, c] = jnp.where(chosen, w - 1.0, w).astype(BF)
+
+    def back(k):
+        c = cols[k]
+        g = jnp.dot(panel_t[...], weights[:, c], preferred_element_type=F32)
+        u = query[:, c].astype(F32)
         inner = jnp.sum(u * g, axis=0, keepdims=True) * (1.0 / width)
-        grad_proj = ((g - u * inner) * (r * mult)).astype(BF)
-        total_w[...] += lax.dot_general(
-            states_t[:, cols], grad_proj, (((1,), (1,)), ((), ())), preferred_element_type=F32
+        grad_p[:, c] = ((g - u * inner) * (scale[:, c] * mult)).astype(BF)
+
+    def weight_part(which, c):
+        return lax.dot_general(
+            states[which, c], grad_p[:, c], (((1,), (1,)), ((), ())), preferred_element_type=F32
         )
 
-    @pl.when(step == pl.num_programs(0) - 1)
-    def _():
-        half_w = width // 2
-        keep[...] = total_w[pl.ds(pl.multiple_of(core[0] * half_w, half_w), half_w), :]
-        rest = total_w[pl.ds(pl.multiple_of((1 - core[0]) * half_w, half_w), half_w), :]
-        give[...] = rest.astype(BF)
-
-
-def losses_and_weights(mult, core, proj, query, scale, label_q, states_t, own, other,
-                       labels, positive, rows):
-    width, queries = proj.shape
+    for copy in panel_in:
+        copy.wait()
+    query_in[0].wait()
+    s = scores(0)
+    panel_t[:, :half] = panel[:half, :].T
+    panel_t[:, half:] = panel[half:, :].T
+    for k in range(count):
+        later = None
+        if k + 1 < count:
+            query_in[k + 1].wait()
+            later = scores(k + 1)
+        if k >= 1:
+            back(k - 1)
+        soften(k, s)
+        s = later
+    for copy in weights_out:
+        copy.start()
+    states_in.wait()
+    early = slice(0, (count - 1) * tile)
+    acc_give[...] = weight_part(theirs, early)
+    acc_keep[...] = weight_part(mine, early)
+    back(count - 1)
+    last = cols[count - 1]
+    give[...] = (acc_give[...] + weight_part(theirs, last)).astype(BF)
+    keep[...] = (acc_keep[...] + weight_part(mine, last)).astype(BF)
+    for copy in weights_out:
+        copy.wait()
+
+
+def losses_and_weights(mult, rows, core, query, scale, label_q, states_t, own, other, labels, positive):
+    width, queries = query.shape
     half = own.shape[0]
     half_w = width // 2
+    count = queries // TILE
+    hbm = pl.BlockSpec(memory_space=pl.ANY)
+    vmem = pl.BlockSpec(memory_space=pltpu.VMEM)
     return pl.pallas_call(
-        functools.partial(loss_kernel, mult, rows),
-        grid=(queries // Q_TILE,),
-        in_specs=[
-            SCALAR, column(width), column(width), column(1), column(1), column(width),
-            whole(own.shape), whole(other.shape), whole(labels.shape), column(1),
-        ],
-        out_specs=[column(1), column(2 * half), whole((half_w, width)), whole((half_w, width))],
+        functools.partial(loss_kernel, mult, rows, TILE),
+        in_specs=[pl.BlockSpec(memory_space=pltpu.SMEM), hbm, hbm, hbm, hbm, vmem, vmem, vmem, vmem],
+        out_specs=[vmem, hbm, vmem, vmem],
         out_shape=[
             jax.ShapeDtypeStruct((1, queries), F32),
             jax.ShapeDtypeStruct((2 * half, queries), BF),
-            jax.ShapeDtypeStruct((half_w, width), F32),
             jax.ShapeDtypeStruct((half_w, width), BF),
+            jax.ShapeDtypeStruct((half_w, width), BF),
         ],
         scratch_shapes=[
-            pltpu.VMEM((width, half), BF),
-            pltpu.VMEM((width, half), BF),
-            pltpu.VMEM((width, width), F32),
+            pltpu.VMEM((2 * half, width), BF),
+            pltpu.VMEM((width, 2 * half), BF),
+            pltpu.VMEM((width, queries), BF),
+            pltpu.VMEM((width, queries), BF),
+            pltpu.VMEM((2 * half, queries), BF),
+            pltpu.VMEM((width, queries), BF),
+            pltpu.VMEM((half_w, width), F32),
+            pltpu.VMEM((half_w, width), F32),
+            pltpu.SemaphoreType.DMA((3 + 2 * count,)),
         ],
         cost_estimate=pl.CostEstimate(
             flops=8 * queries * width * half + 2 * queries * width * width,
-            bytes_accessed=queries * width * 12,
+            bytes_accessed=queries * width * 8,
             transcendentals=2 * half * queries,
         ),
         name="losses",
-    )(core, proj, query, scale, label_q, states_t, own, other, labels, positive)
+    )(core, query, states_t, own, other, scale, label_q, labels, positive)
 
 
 def on_device(states, query_weight, attempts, attempt_theorem, positive):
@@ -234,14 +262,16 @@
     labels = labels.reshape(-1, 1)
     pos = positive.reshape(1, -1)
 
-    proj, query, scale, label_q, states_t = project(core, states, query_weight, labels, pos, rows)
+    query, scale, label_q, states_t = project(
+        core, states, query_weight, labels, pos, rows
+    )
     loss, weights, w_keep, w_give = losses_and_weights(
-        mult, core, proj, query, scale, label_q, states_t, own, other, labels, pos, rows
+        mult, rows, core, query, scale, label_q, states_t, own, other, labels, pos
     )
 
     half_a = own.shape[0]
     contract = (((1,), (1,)), ((), ()))
-    w_sum = (w_keep + to_core(w_give).astype(F32)).astype(BF)
+    w_sum = (w_keep.astype(F32) + to_core(w_give).astype(F32)).astype(BF)
     parts = lax.all_to_all(w_sum.reshape(16, -1, width), PLANE, 0, 0)
     a_give = lax.dot_general(
         weights[half_a:], query, contract, preferred_element_type=F32

time: 128 us -> 124 us (0.969)
  Pallas kernels: 30.4 us -> 26.4 us
    pallas_call x1, Pallas kernels: 19.3 us -> 16.4 us  [losses_and_weights(): pl.pallas_call(functools.partial(loss_kernel, mult, rows, TILE), in_specs...]
where the time goes in v1:
time: 124 us; the launch traced here: 123 us
  waiting for transfers between devices  29.6 us (24%)
  starting transfers between devices  27.5 us (22%)
  Pallas kernels  26.4 us (21%)
  blocking collectives  20.7 us (17%)
  matrix products  9.59 us (8%)
  other arithmetic  5.74 us (5%)
  local copies, waits for them, and re-layouts  3.01 us (2%)
    all_to_all x1, blocking collectives, on_device(): own = lax.all_to_all(spread_a, ROW, 0, 0).reshape(-1, width)  20.7 us
    pallas_call x1, Pallas kernels, losses_and_weights(): pl.pallas_call(functools.partial(loss_kernel, mult, rows, TILE), in_specs...  16.4 us
    ppermute x8, starting transfers between devices, send(): return lax.ppermute(value, AXES, pairs)  13.3 us
    all_to_all x1, waiting for transfers between devices, on_device(): a_parts = lax.all_to_all(a_sum.reshape(8, rows, width), ROW, 0, 0)  10.3 us
    ppermute x8, waiting for transfers between devices, send(): return lax.ppermute(value, AXES, pairs)  8.15 us
    pallas_call x1, Pallas kernels, project(): pl.pallas_call(functools.partial(proj_kernel, rows), grid=(queries // Q_T...  8.13 us
    all_to_all x1, waiting for transfers between devices, on_device(): parts = lax.all_to_all(w_sum.reshape(16, -1, width), PLANE, 0, 0)  7.25 us
    dot_general x1, matrix products, on_device(): lax.dot_general(weights[:half_a], query, contract, preferred_element_type...  5.23 us
  transfers between devices with their start and end apart: 11, of which 7 were waited for; matrix products, arithmetic and copies ran while one was open for 11% of the time, Pallas kernels for 7%

profile of v1, /device:TPU:2, one launch (start us, length us, event | category | flops | bytes accessed | tf_op | source)
XLA Modules:
  0.0 123.3 jit_solution(15969667061524327611)
XLA Ops:
  0.6 1.9 %unit.1 = (bf16[8,64,768]{2,1,0:T(8,128)(2,1)}, f32[64,1]{1,0:T(8,128)}) custom-call(bf16[64,768]{1,0:T(8,128)(2,1)} %attempts.1), custom_call_target="tpu_custom_call" | custom-call | flops 196608 | bytes 884736 | tf_op jit(solution)/shard_map/unit/pallas_call | solution.py:55
  2.6 20.7 %all_to_all.20 = bf16[8,64,768]{2,1,0:T(8,128)(2,1)S(1)} all-to-all(bf16[8,64,768]{2,1,0:T(8,128)(2,1)} %get-tuple-element.15), channel_id=1, replica_groups=mesh['z'=8,'yl'=2,'yh'=2,'x'=4,'c'=2] {'yh','x'}, dimensions={0} | all-to-all | bytes 1572864 | tf_op jit(solution)/shard_map/all_to_all | solution.py:256
  23.3 0.7 convert_element_type.56
  24.3 1.1 copy.8.labels
  25.3 8.1 %project.1 = (bf16[768,2048]{1,0:T(8,128)(2,1)}, f32[1,2048]{1,0:T(1,128)}, f32[1,2048]{1,0:T(1,128)}, bf16[768,2048]{1,0:T(8,128)(2,1)}) custom-call(s32[1]{0:T(128)} %bitcast.core, bf16[2048,768]{1,0:T(8,128)(2,1)} %states.1, bf16[768,768]{1,0:T(8,128)(2,1)} %weight.1, f32[1024,1]{1,0:T(8,128)} %copy.8.labels, s32[1,2048]{1,0:T(1,128)} %bitcast.16), custom_call_target="tpu_custom_call" | custom-call | flops 2415919104 | bytes 9437184 | tf_op jit(solution)/shard_map/project/pallas_call | solution.py:104
  33.5 0.9 copy-done.3
  34.3 16.4 %losses.1 = (f32[1,2048]{1,0:T(1,128)}, bf16[1024,2048]{1,0:T(8,128)(2,1)}, bf16[384,768]{1,0:T(8,128)(2,1)}, bf16[384,768]{1,0:T(8,128)(2,1)}) custom-call(s32[1]{0:T(128)} %bitcast.core, bf16[768,2048]{1,0:T(8,128)(2,1)} %get-tuple-element.13.query_hbm, bf16[768,2048]{1,0:T(8,128)(2,1)} %get-tuple-element.14.states_hbm, bf16[512,768]{1,0:T(8,128)(2,1)} %bitcast.14, ...), custom_call_target="tpu_custom_call" | custom-call | flops 8858370048 | bytes 12582912 | tf_op jit(solution)/shard_map/losses/pallas_call | solution.py:218
  50.7 0.8 collective-permute-start.2
  51.5 1.8 %collective-permute-done.2 = bf16[384,768]{1,0:T(8,128)(2,1)S(1)} collective-permute-done((bf16[384,768]{1,0:T(8,128)(2,1)}, bf16[384,768]{1,0:T(8,128)(2,1)S(1)}, u32[]{:S(2)}, u32[]{:S(2)}) %collective-permute-start.2) | collective-permute-done | bytes 589856 | tf_op jit(solution)/shard_map/ppermute | solution.py:33
  53.4 2.0 %add_convert_fusion.1 = bf16[384,768]{1,0:T(8,128)(2,1)} fusion(bf16[384,768]{1,0:T(8,128)(2,1)S(1)} %collective-permute-done.2, bf16[384,768]{1,0:T(8,128)(2,1)} %get-tuple-element.21), kind=kLoop, calls=%fused_computation.8 | loop fusion | flops 1179648 | bytes 1769472 | tf_op jit(solution)/shard_map/convert_element_type | solution.py:274
  55.4 4.5 %all-to-all-start.2 = ((bf16[16,24,768]{2,1,0:T(8,128)(2,1)}), bf16[16,24,768]{2,1,0:T(8,128)(2,1)S(1)}, u32[]{:S(2)}, u32[]{:S(2)}) async-start(bf16[16,24,768]{2,1,0:T(8,128)(2,1)} %bitcast.6), calls=%async_computation.2 | async-start | bytes 1179648 | tf_op jit(solution)/shard_map/all_to_all | solution.py:275
  59.9 4.4 %fusion.6 = bf16[512,768]{1,0:T(8,128)(2,1)S(1)} fusion(bf16[768,2048]{1,0:T(8,128)(2,1)} %get-tuple-element.13.query_hbm, bf16[1024,2048]{1,0:T(8,128)(2,1)} %get-tuple-element.19), kind=kOutput, calls=%fused_computation.6 | convolution fusion | flops 1611005952 | bytes 6029312 | tf_op jit(solution)/shard_map/dot_general | solution.py:276
  64.2 0.2 collective-permute-start.1
  64.4 7.2 %all-to-all-done.2 = bf16[16,24,768]{2,1,0:T(8,128)(2,1)S(1)} async-done(((bf16[16,24,768]{2,1,0:T(8,128)(2,1)}), bf16[16,24,768]{2,1,0:T(8,128)(2,1)S(1)}, u32[]{:S(2)}, u32[]{:S(2)}) %all-to-all-start.2) | async-done | bytes 589856 | tf_op jit(solution)/shard_map/all_to_all | solution.py:275
  71.7 2.0 %collective-permute-start.3 = (bf16[24,768]{1,0:T(8,128)(2,1)S(1)}, bf16[24,768]{1,0:T(8,128)(2,1)S(1)}, u32[]{:S(2)}, u32[]{:S(2)}) collective-permute-start(bf16[24,768]{1,0:T(8,128)(2,1)S(1)} %reduce_sum.32), channel_id=1, source_target_pairs={{0,32},{1,33},{2,34},{3,35},{4,36},{5,37},{6,38},{7,39},{8,40},{9,... | collective-permute-start | bytes 110600 | tf_op jit(solution)/shard_map/ppermute | solution.py:33
  73.7 2.0 %collective-permute-done.3 = bf16[24,768]{1,0:T(8,128)(2,1)S(1)} collective-permute-done((bf16[24,768]{1,0:T(8,128)(2,1)S(1)}, bf16[24,768]{1,0:T(8,128)(2,1)S(1)}, u32[]{:S(2)}, u32[]{:S(2)}) %collective-permute-start.3) | collective-permute-done | bytes 36896 | tf_op jit(solution)/shard_map/ppermute | solution.py:33
  75.8 6.4 %collective-permute-start.6 = (bf16[24,768]{1,0:T(8,128)(2,1)S(1)}, bf16[24,768]{1,0:T(8,128)(2,1)S(1)}, u32[]{:S(2)}, u32[]{:S(2)}) collective-permute-start(bf16[24,768]{1,0:T(8,128)(2,1)S(1)} %add_convert_fusion.3), channel_id=1, source_target_pairs={{0,192},{1,193},{2,194},{3,195},{4,196},{5,197},{6,198},{7,199},{8... | collective-permute-start | bytes 110600 | tf_op jit(solution)/shard_map/ppermute | solution.py:33
  82.2 3.8 %collective-permute-start.4 = (bf16[24,768]{1,0:T(8,128)(2,1)S(1)}, bf16[24,768]{1,0:T(8,128)(2,1)S(1)}, u32[]{:S(2)}, u32[]{:S(2)}) collective-permute-start(bf16[24,768]{1,0:T(8,128)(2,1)S(1)} %add_convert_fusion.3), channel_id=1, source_target_pairs={{0,128},{1,129},{2,130},{3,131},{4,132},{5,133},{6,134},{7,135},{8... | collective-permute-start | bytes 110600 | tf_op jit(solution)/shard_map/ppermute | solution.py:33
  86.0 2.2 %collective-permute-done.5 = bf16[24,768]{1,0:T(8,128)(2,1)S(1)} collective-permute-done((bf16[24,768]{1,0:T(8,128)(2,1)S(1)}, bf16[24,768]{1,0:T(8,128)(2,1)S(1)}, u32[]{:S(2)}, u32[]{:S(2)}) %collective-permute-start.5) | collective-permute-done | bytes 36896 | tf_op jit(solution)/shard_map/ppermute | solution.py:33
  88.2 2.0 %collective-permute-done.4 = bf16[24,768]{1,0:T(8,128)(2,1)S(1)} collective-permute-done((bf16[24,768]{1,0:T(8,128)(2,1)S(1)}, bf16[24,768]{1,0:T(8,128)(2,1)S(1)}, u32[]{:S(2)}, u32[]{:S(2)}) %collective-permute-start.4) | collective-permute-done | bytes 36896 | tf_op jit(solution)/shard_map/ppermute | solution.py:33
  90.3 0.8 broadcast_in_dim.2
  91.1 4.8 %all-to-all-start.3 = ((bf16[16,24,768]{2,1,0:T(8,128)(2,1)}), bf16[16,24,768]{2,1,0:T(8,128)(2,1)S(1)}, u32[]{:S(2)}, u32[]{:S(2)}) async-start(bf16[16,24,768]{2,1,0:T(8,128)(2,1)} %broadcast_in_dim.2), calls=%async_computation.3 | async-start | bytes 1179648 | tf_op jit(solution)/shard_map/all_to_all | solution.py:296
  96.0 5.2 %add_convert_fusion = bf16[512,768]{1,0:T(8,128)(2,1)} fusion(bf16[512,768]{1,0:T(8,128)(2,1)S(1)} %collective-permute-done.1, bf16[768,2048]{1,0:T(8,128)(2,1)} %get-tuple-element.13.query_hbm, bf16[1024,2048]{1,0:T(8,128)(2,1)} %get-tuple-element.19), kind=kOutput, calls=%fused_computation.5 | convolution fusion | flops 1611792384 | bytes 6815744 | tf_op jit(solution)/shard_map/dot_general | solution.py:279
  101.2 4.0 %all-to-all-done.3 = bf16[16,24,768]{2,1,0:T(8,128)(2,1)S(1)} async-done(((bf16[16,24,768]{2,1,0:T(8,128)(2,1)}), bf16[16,24,768]{2,1,0:T(8,128)(2,1)S(1)}, u32[]{:S(2)}, u32[]{:S(2)}) %all-to-all-start.3) | async-done | bytes 589856 | tf_op jit(solution)/shard_map/all_to_all | solution.py:296
  105.2 4.9 %all-to-all-start.1 = ((bf16[8,64,768]{2,1,0:T(8,128)(2,1)}), bf16[8,64,768]{2,1,0:T(8,128)(2,1)S(1)}, u32[]{:S(2)}, u32[]{:S(2)}) async-start(bf16[8,64,768]{2,1,0:T(8,128)(2,1)} %bitcast.5), calls=%async_computation.1 | async-start | bytes 1572864 | tf_op jit(solution)/shard_map/all_to_all | solution.py:283
  110.1 0.1 fusion.11
  110.3 10.3 %all-to-all-done.1 = bf16[8,64,768]{2,1,0:T(8,128)(2,1)S(1)} async-done(((bf16[8,64,768]{2,1,0:T(8,128)(2,1)}), bf16[8,64,768]{2,1,0:T(8,128)(2,1)S(1)}, u32[]{:S(2)}, u32[]{:S(2)}) %all-to-all-start.1) | async-done | bytes 786464 | tf_op jit(solution)/shard_map/all_to_all | solution.py:283
  120.6 0.1 convert_reduce_fusion
  120.7 0.2 multiply_reduce_fusion
  120.9 0.8 subtract_multiply_fusion
  121.6 0.1 broadcast_select_fusion.1
  121.8 1.6 %maximum_convert_fusion = f32[768,768]{1,0:T(8,128)} fusion(bf16[384,768]{1,0:T(8,128)(2,1)S(1)} %get-tuple-element.28, bf16[384,768]{1,0:T(8,128)(2,1)S(1)} %get-tuple-element.27), kind=kLoop, calls=%fused_computation.7 | loop fusion | flops 2359296 | bytes 3538944 | tf_op jit(solution)/shard_map/convert_element_type | solution.py:300
  (23 shorter events, 0.5 us)
Async XLA Ops:
  23.3 10.2 %copy-start.1 = (bf16[8,64,768]{2,1,0:T(8,128)(2,1)}, bf16[8,64,768]{2,1,0:T(8,128)(2,1)S(1)}, u32[]{:S(2)}) copy-start(bf16[8,64,768]{2,1,0:T(8,128)(2,1)S(1)} %all_to_all.20) | copy-start | bytes 2359300
  23.3 10.2 %collective-permute-start = (bf16[512,768]{1,0:T(8,128)(2,1)S(1)}, bf16[512,768]{1,0:T(8,128)(2,1)S(1)}, u32[]{:S(2)}, u32[]{:S(2)}) collective-permute-start(bf16[512,768]{1,0:T(8,128)(2,1)S(1)} %bitcast.13), channel_id=1, source_target_pairs={{0,1},{1,0},{2,3},{3,2},{4,5},{5,4},{6,7},{7,6},{8,9},{9,8},{10,11... | collective-permute-start | bytes 2359304 | tf_op jit(solution)/shard_map/ppermute | solution.py:33
  33.5 0.9 copy-start.3
  50.7 2.6 %collective-permute-start.2 = (bf16[384,768]{1,0:T(8,128)(2,1)}, bf16[384,768]{1,0:T(8,128)(2,1)S(1)}, u32[]{:S(2)}, u32[]{:S(2)}) collective-permute-start(bf16[384,768]{1,0:T(8,128)(2,1)} %get-tuple-element.22), channel_id=1, source_target_pairs={{0,1},{1,0},{2,3},{3,2},{4,5},{5,4},{6,7},{7,6},{8,9},{9,8},{10,11... | collective-permute-start | bytes 1769480 | tf_op jit(solution)/shard_map/ppermute | solution.py:33
  55.4 16.3 %all-to-all-start.2 = ((bf16[16,24,768]{2,1,0:T(8,128)(2,1)}), bf16[16,24,768]{2,1,0:T(8,128)(2,1)S(1)}, u32[]{:S(2)}, u32[]{:S(2)}) async-start(bf16[16,24,768]{2,1,0:T(8,128)(2,1)} %bitcast.6), calls=%async_computation.2 | async-start | bytes 1179648 | tf_op jit(solution)/shard_map/all_to_all | solution.py:275
  64.2 31.8 %collective-permute-start.1 = (bf16[512,768]{1,0:T(8,128)(2,1)S(1)}, bf16[512,768]{1,0:T(8,128)(2,1)S(1)}, u32[]{:S(2)}, u32[]{:S(2)}) collective-permute-start(bf16[512,768]{1,0:T(8,128)(2,1)S(1)} %fusion.6), channel_id=1, source_target_pairs={{0,1},{1,0},{2,3},{3,2},{4,5},{5,4},{6,7},{7,6},{8,9},{9,8},{10,11... | collective-permute-start | bytes 2359304 | tf_op jit(solution)/shard_map/ppermute | solution.py:33
  71.7 4.0 %collective-permute-start.3 = (bf16[24,768]{1,0:T(8,128)(2,1)S(1)}, bf16[24,768]{1,0:T(8,128)(2,1)S(1)}, u32[]{:S(2)}, u32[]{:S(2)}) collective-permute-start(bf16[24,768]{1,0:T(8,128)(2,1)S(1)} %reduce_sum.32), channel_id=1, source_target_pairs={{0,32},{1,33},{2,34},{3,35},{4,36},{5,37},{6,38},{7,39},{8,40},{9,... | collective-permute-start | bytes 110600 | tf_op jit(solution)/shard_map/ppermute | solution.py:33
  75.8 10.2 %collective-permute-start.6 = (bf16[24,768]{1,0:T(8,128)(2,1)S(1)}, bf16[24,768]{1,0:T(8,128)(2,1)S(1)}, u32[]{:S(2)}, u32[]{:S(2)}) collective-permute-start(bf16[24,768]{1,0:T(8,128)(2,1)S(1)} %add_convert_fusion.3), channel_id=1, source_target_pairs={{0,192},{1,193},{2,194},{3,195},{4,196},{5,197},{6,198},{7,199},{8... | collective-permute-start | bytes 110600 | tf_op jit(solution)/shard_map/ppermute | solution.py:33
  82.2 6.1 %collective-permute-start.5 = (bf16[24,768]{1,0:T(8,128)(2,1)S(1)}, bf16[24,768]{1,0:T(8,128)(2,1)S(1)}, u32[]{:S(2)}, u32[]{:S(2)}) collective-permute-start(bf16[24,768]{1,0:T(8,128)(2,1)S(1)} %add_convert_fusion.3), channel_id=1, source_target_pairs={{0,64},{1,65},{2,66},{3,67},{4,68},{5,69},{6,70},{7,71},{8,72},{9,... | collective-permute-start | bytes 110600 | tf_op jit(solution)/shard_map/ppermute | solution.py:33
  82.2 8.1 %collective-permute-start.4 = (bf16[24,768]{1,0:T(8,128)(2,1)S(1)}, bf16[24,768]{1,0:T(8,128)(2,1)S(1)}, u32[]{:S(2)}, u32[]{:S(2)}) collective-permute-start(bf16[24,768]{1,0:T(8,128)(2,1)S(1)} %add_convert_fusion.3), channel_id=1, source_target_pairs={{0,128},{1,129},{2,130},{3,131},{4,132},{5,133},{6,134},{7,135},{8... | collective-permute-start | bytes 110600 | tf_op jit(solution)/shard_map/ppermute | solution.py:33
  91.1 14.0 %all-to-all-start.3 = ((bf16[16,24,768]{2,1,0:T(8,128)(2,1)}), bf16[16,24,768]{2,1,0:T(8,128)(2,1)S(1)}, u32[]{:S(2)}, u32[]{:S(2)}) async-start(bf16[16,24,768]{2,1,0:T(8,128)(2,1)} %broadcast_in_dim.2), calls=%async_computation.3 | async-start | bytes 1179648 | tf_op jit(solution)/shard_map/all_to_all | solution.py:296
  96.0 14.1 %copy-start.2 = (f32[64,1]{1,0:T(8,128)S(1)}, f32[64,1]{1,0:T(8,128)}, u32[]{:S(2)}) copy-start(f32[64,1]{1,0:T(8,128)} %get-tuple-element.20) | copy-start | bytes 772
  101.2 19.4 %copy-start = (bf16[64,768]{1,0:T(8,128)(2,1)S(1)}, bf16[64,768]{1,0:T(8,128)(2,1)}, u32[]{:S(2)}) copy-start(bf16[64,768]{1,0:T(8,128)(2,1)} %attempts.1) | copy-start | bytes 294916
  105.2 15.4 %all-to-all-start.1 = ((bf16[8,64,768]{2,1,0:T(8,128)(2,1)}), bf16[8,64,768]{2,1,0:T(8,128)(2,1)S(1)}, u32[]{:S(2)}, u32[]{:S(2)}) async-start(bf16[8,64,768]{2,1,0:T(8,128)(2,1)} %bitcast.5), calls=%async_computation.1 | async-start | bytes 1572864 | tf_op jit(solution)/shard_map/all_to_all | solution.py:283
  110.2 11.5 %collective-permute-start.7 = (bf16[384,768]{1,0:T(8,128)(2,1)S(1)}, bf16[384,768]{1,0:T(8,128)(2,1)S(1)}, u32[]{:S(2)}, u32[]{:S(2)}) collective-permute-start(bf16[384,768]{1,0:T(8,128)(2,1)S(1)} %bitcast.12), channel_id=1, source_target_pairs={{0,1},{1,0},{2,3},{3,2},{4,5},{5,4},{6,7},{7,6},{8,9},{9,8},{10,11... | collective-permute-start | bytes 1769480 | tf_op jit(solution)/shard_map/ppermute | solution.py:33

commit v2 on v1

--- a/solution.py
+++ b/solution.py
@@ -126,27 +126,23 @@
     )(core, states, weight, labels, positive)
 
 
-def loss_kernel(mult, rows, tile, core, query_hbm, states_hbm, own_hbm, other_hbm, scale, label_q, labels,
+def loss_kernel(mult, rows, tile, core, query_hbm, states_hbm, own, other, scale, label_q, labels,
                  positive, loss, weights_hbm, keep, give,
                  panel, panel_t, query, states, weights, grad_p, acc_keep, acc_give, sems):
-    half, width = own_hbm.shape
+    half, width = own.shape
     queries = query_hbm.shape[1]
     count = queries // tile
     cols = [slice(k * tile, (k + 1) * tile) for k in range(count)]
-    panel_in = [
-        pltpu.make_async_copy(own_hbm, panel.at[:half, :], sems.at[0]),
-        pltpu.make_async_copy(other_hbm, panel.at[half:, :], sems.at[1]),
-    ]
     query_in = [
-        pltpu.make_async_copy(query_hbm.at[:, c], query.at[:, c], sems.at[2 + k])
+        pltpu.make_async_copy(query_hbm.at[:, c], query.at[:, c], sems.at[k])
         for k, c in enumerate(cols)
     ]
-    states_in = pltpu.make_async_copy(states_hbm, states, sems.at[2 + count])
+    states_in = pltpu.make_async_copy(states_hbm, states, sems.at[count])
     weights_out = [
-        pltpu.make_async_copy(weights.at[:, c], weights_hbm.at[:, c], sems.at[3 + count + k])
+        pltpu.make_async_copy(weights.at[:, c], weights_hbm.at[:, c], sems.at[1 + count + k])
         for k, c in enumerate(cols)
     ]
-    for copy in panel_in + query_in + [states_in]:
+    for copy in query_in + [states_in]:
         copy.start()
     ids = jnp.concatenate([row_ids(core[0], half, rows), row_ids(1 - core[0], half, rows)], axis=0)
     label_j = labels[...]
@@ -179,12 +175,12 @@
             states[which, c], grad_p[:, c], (((1,), (1,)), ((), ())), preferred_element_type=F32
         )
 
-    for copy in panel_in:
-        copy.wait()
+    panel[:half, :] = own[...]
+    panel[half:, :] = other[...]
     query_in[0].wait()
     s = scores(0)
-    panel_t[:, :half] = panel[:half, :].T
-    panel_t[:, half:] = panel[half:, :].T
+    panel_t[:, :half] = own[...].T
+    panel_t[:, half:] = other[...].T
     for k in range(count):
         later = None
         if k + 1 < count:
@@ -217,7 +213,7 @@
     vmem = pl.BlockSpec(memory_space=pltpu.VMEM)
     return pl.pallas_call(
         functools.partial(loss_kernel, mult, rows, TILE),
-        in_specs=[pl.BlockSpec(memory_space=pltpu.SMEM), hbm, hbm, hbm, hbm, vmem, vmem, vmem, vmem],
+        in_specs=[pl.BlockSpec(memory_space=pltpu.SMEM), hbm, hbm, vmem, vmem, vmem, vmem, vmem, vmem],
         out_specs=[vmem, hbm, vmem, vmem],
         out_shape=[
             jax.ShapeDtypeStruct((1, queries), F32),
@@ -234,13 +230,14 @@
             pltpu.VMEM((width, queries), BF),
             pltpu.VMEM((half_w, width), F32),
             pltpu.VMEM((half_w, width), F32),
-            pltpu.SemaphoreType.DMA((3 + 2 * count,)),
+            pltpu.SemaphoreType.DMA((1 + 2 * count,)),
         ],
         cost_estimate=pl.CostEstimate(
             flops=8 * queries * width * half + 2 * queries * width * width,
             bytes_accessed=queries * width * 8,
             transcendentals=2 * half * queries,
         ),
+        compiler_params=pltpu.CompilerParams(vmem_limit_bytes=44 * 2**20),
         name="losses",
     )(core, query, states_t, own, other, scale, label_q, labels, positive)
 

time: 124 us -> 125 us (level)
  local copies, waits for them, and re-layouts: 3.01 us -> 7.29 us
  Pallas kernels: 26.4 us -> 24.6 us
    unnamed x8 -> x16, local copies, waits for them, and re-layouts: 0.88 us -> 5.18 us
    pallas_call x1, Pallas kernels: 16.4 us -> 14.4 us  [losses_and_weights(): pl.pallas_call(functools.partial(loss_kernel, mult, rows, TILE), in_specs...]
  transfers between devices with their start and end apart: 11 -> 11, of which waited for: 7 -> 7; matrix products, arithmetic and copies ran while one was open for 11% -> 12% of each run, Pallas kernels for 7% -> 7%
where the time goes in v2:
time: 125 us; the launch traced here: 124 us
  waiting for transfers between devices  28.6 us (23%)
  starting transfers between devices  27.2 us (22%)
  Pallas kernels  24.6 us (20%)
  blocking collectives  20.7 us (17%)
  matrix products  10.5 us (8%)
  local copies, waits for them, and re-layouts  7.29 us (6%)
  other arithmetic  4.67 us (4%)
    all_to_all x1, blocking collectives, on_device(): own = lax.all_to_all(spread_a, ROW, 0, 0).reshape(-1, width)  20.7 us
    pallas_call x1, Pallas kernels, losses_and_weights(): pl.pallas_call(functools.partial(loss_kernel, mult, rows, TILE), in_specs...  14.4 us
    ppermute x8, starting transfers between devices, send(): return lax.ppermute(value, AXES, pairs)  13 us
    all_to_all x1, waiting for transfers between devices, on_device(): a_parts = lax.all_to_all(a_sum.reshape(8, rows, width), ROW, 0, 0)  10.3 us
    pallas_call x1, Pallas kernels, project(): pl.pallas_call(functools.partial(proj_kernel, rows), grid=(queries // Q_T...  8.19 us
    ppermute x8, waiting for transfers between devices, send(): return lax.ppermute(value, AXES, pairs)  7.97 us
    all_to_all x1, waiting for transfers between devices, on_device(): parts = lax.all_to_all(w_sum.reshape(16, -1, width), PLANE, 0, 0)  6.45 us
    dot_general x1, matrix products, on_device(): lax.dot_general(weights[:half_a], query, contract, preferred_element_type...  5.24 us
  transfers between devices with their start and end apart: 11, of which 7 were waited for; matrix products, arithmetic and copies ran while one was open for 12% of the time, Pallas kernels for 7%

profile of v2, /device:TPU:2, one launch (start us, length us, event | category | flops | bytes accessed | tf_op | source)
XLA Modules:
  0.0 124.3 jit_solution(12209540247135092620)
XLA Ops:
  0.6 1.9 %unit.1 = (bf16[8,64,768]{2,1,0:T(8,128)(2,1)}, f32[64,1]{1,0:T(8,128)}) custom-call(bf16[64,768]{1,0:T(8,128)(2,1)} %attempts.1), custom_call_target="tpu_custom_call" | custom-call | flops 196608 | bytes 884736 | tf_op jit(solution)/shard_map/unit/pallas_call | solution.py:55
  2.6 20.7 %all_to_all.20 = bf16[8,64,768]{2,1,0:T(8,128)(2,1)S(1)} all-to-all(bf16[8,64,768]{2,1,0:T(8,128)(2,1)} %get-tuple-element.15), channel_id=1, replica_groups=mesh['z'=8,'yl'=2,'yh'=2,'x'=4,'c'=2] {'yh','x'}, dimensions={0} | all-to-all | bytes 1572864 | tf_op jit(solution)/shard_map/all_to_all | solution.py:253
  23.3 0.7 convert_element_type.56
  24.3 1.0 copy.8.labels
  25.3 8.2 %project.1 = (bf16[768,2048]{1,0:T(8,128)(2,1)}, f32[1,2048]{1,0:T(1,128)}, f32[1,2048]{1,0:T(1,128)}, bf16[768,2048]{1,0:T(8,128)(2,1)}) custom-call(s32[1]{0:T(128)} %bitcast.core, bf16[2048,768]{1,0:T(8,128)(2,1)} %states.1, bf16[768,768]{1,0:T(8,128)(2,1)} %weight.1, f32[1024,1]{1,0:T(8,128)} %copy.8.labels, s32[1,2048]{1,0:T(1,128)} %bitcast.14), custom_call_target="tpu_custom_call" | custom-call | flops 2415919104 | bytes 9437184 | tf_op jit(solution)/shard_map/project/pallas_call | solution.py:104
  33.5 1.9 %copy-done.2 = bf16[768,2048]{1,0:T(8,128)(2,1)S(1)} copy-done((bf16[768,2048]{1,0:T(8,128)(2,1)S(1)}, bf16[768,2048]{1,0:T(8,128)(2,1)}, u32[]{:S(2)}) %copy-start.2) | copy-done | bytes 3145752
  35.4 1.9 %copy-done.3 = bf16[768,2048]{1,0:T(8,128)(2,1)S(1)} copy-done((bf16[768,2048]{1,0:T(8,128)(2,1)S(1)}, bf16[768,2048]{1,0:T(8,128)(2,1)}, u32[]{:S(2)}) %copy-start.3) | copy-done | bytes 3145752
  37.3 0.7 copy-done.4
  38.0 0.7 copy-done.5
  38.7 14.4 %losses.1 = (f32[1,2048]{1,0:T(1,128)}, bf16[1024,2048]{1,0:T(8,128)(2,1)}, bf16[384,768]{1,0:T(8,128)(2,1)S(1)}, bf16[384,768]{1,0:T(8,128)(2,1)S(1)}) custom-call(s32[1]{0:T(128)} %bitcast.core, bf16[768,2048]{1,0:T(8,128)(2,1)S(1)} %copy-done.2, bf16[768,2048]{1,0:T(8,128)(2,1)S(1)} %copy-done.3, bf16[512,768]{1,0:T(8,128)(2,1)S(1)} %bitcast.13, ...), custom_call_target="tpu_custom_call" | custom-call | flops 8858370048 | bytes 12582912 | tf_op jit(solution)/shard_map/losses/pallas_call | solution.py:214
  53.1 0.6 collective-permute-start.2
  53.7 1.6 %collective-permute-done.2 = bf16[384,768]{1,0:T(8,128)(2,1)S(1)} collective-permute-done((bf16[384,768]{1,0:T(8,128)(2,1)S(1)}, bf16[384,768]{1,0:T(8,128)(2,1)S(1)}, u32[]{:S(2)}, u32[]{:S(2)}) %collective-permute-start.2) | collective-permute-done | bytes 589856 | tf_op jit(solution)/shard_map/ppermute | solution.py:33
  55.4 1.0 add_convert_fusion.1
  56.3 4.5 %all-to-all-start.2 = ((bf16[16,24,768]{2,1,0:T(8,128)(2,1)}), bf16[16,24,768]{2,1,0:T(8,128)(2,1)S(1)}, u32[]{:S(2)}, u32[]{:S(2)}) async-start(bf16[16,24,768]{2,1,0:T(8,128)(2,1)} %bitcast.6), calls=%async_computation.2 | async-start | bytes 1179648 | tf_op jit(solution)/shard_map/all_to_all | solution.py:272
  60.8 5.2 %fusion.6 = bf16[512,768]{1,0:T(8,128)(2,1)} fusion(bf16[768,2048]{1,0:T(8,128)(2,1)} %get-tuple-element.13.query_hbm, bf16[1024,2048]{1,0:T(8,128)(2,1)} %get-tuple-element.19), kind=kOutput, calls=%fused_computation.6 | convolution fusion | flops 1611005952 | bytes 6029312 | tf_op jit(solution)/shard_map/dot_general | solution.py:273
  66.1 6.5 %all-to-all-done.2 = bf16[16,24,768]{2,1,0:T(8,128)(2,1)S(1)} async-done(((bf16[16,24,768]{2,1,0:T(8,128)(2,1)}), bf16[16,24,768]{2,1,0:T(8,128)(2,1)S(1)}, u32[]{:S(2)}, u32[]{:S(2)}) %all-to-all-start.2) | async-done | bytes 589856 | tf_op jit(solution)/shard_map/all_to_all | solution.py:272
  72.7 2.0 %collective-permute-start.3 = (bf16[24,768]{1,0:T(8,128)(2,1)S(1)}, bf16[24,768]{1,0:T(8,128)(2,1)S(1)}, u32[]{:S(2)}, u32[]{:S(2)}) collective-permute-start(bf16[24,768]{1,0:T(8,128)(2,1)S(1)} %reduce_sum.32), channel_id=1, source_target_pairs={{0,32},{1,33},{2,34},{3,35},{4,36},{5,37},{6,38},{7,39},{8,40},{9,... | collective-permute-start | bytes 110600 | tf_op jit(solution)/shard_map/ppermute | solution.py:33
  74.7 2.0 %collective-permute-done.3 = bf16[24,768]{1,0:T(8,128)(2,1)S(1)} collective-permute-done((bf16[24,768]{1,0:T(8,128)(2,1)S(1)}, bf16[24,768]{1,0:T(8,128)(2,1)S(1)}, u32[]{:S(2)}, u32[]{:S(2)}) %collective-permute-start.3) | collective-permute-done | bytes 36896 | tf_op jit(solution)/shard_map/ppermute | solution.py:33
  76.7 6.4 %collective-permute-start.6 = (bf16[24,768]{1,0:T(8,128)(2,1)S(1)}, bf16[24,768]{1,0:T(8,128)(2,1)S(1)}, u32[]{:S(2)}, u32[]{:S(2)}) collective-permute-start(bf16[24,768]{1,0:T(8,128)(2,1)S(1)} %add_convert_fusion.3), channel_id=1, source_target_pairs={{0,192},{1,193},{2,194},{3,195},{4,196},{5,197},{6,198},{7,199},{8... | collective-permute-start | bytes 110600 | tf_op jit(solution)/shard_map/ppermute | solution.py:33
  83.1 3.8 %collective-permute-start.4 = (bf16[24,768]{1,0:T(8,128)(2,1)S(1)}, bf16[24,768]{1,0:T(8,128)(2,1)S(1)}, u32[]{:S(2)}, u32[]{:S(2)}) collective-permute-start(bf16[24,768]{1,0:T(8,128)(2,1)S(1)} %add_convert_fusion.3), channel_id=1, source_target_pairs={{0,128},{1,129},{2,130},{3,131},{4,132},{5,133},{6,134},{7,135},{8... | collective-permute-start | bytes 110600 | tf_op jit(solution)/shard_map/ppermute | solution.py:33
  86.9 2.3 %collective-permute-done.5 = bf16[24,768]{1,0:T(8,128)(2,1)S(1)} collective-permute-done((bf16[24,768]{1,0:T(8,128)(2,1)S(1)}, bf16[24,768]{1,0:T(8,128)(2,1)S(1)}, u32[]{:S(2)}, u32[]{:S(2)}) %collective-permute-start.5) | collective-permute-done | bytes 36896 | tf_op jit(solution)/shard_map/ppermute | solution.py:33
  89.2 2.0 %collective-permute-done.4 = bf16[24,768]{1,0:T(8,128)(2,1)S(1)} collective-permute-done((bf16[24,768]{1,0:T(8,128)(2,1)S(1)}, bf16[24,768]{1,0:T(8,128)(2,1)S(1)}, u32[]{:S(2)}, u32[]{:S(2)}) %collective-permute-start.4) | collective-permute-done | bytes 36896 | tf_op jit(solution)/shard_map/ppermute | solution.py:33
  91.2 0.9 broadcast_in_dim.2
  92.1 4.8 %all-to-all-start.3 = ((bf16[16,24,768]{2,1,0:T(8,128)(2,1)}), bf16[16,24,768]{2,1,0:T(8,128)(2,1)S(1)}, u32[]{:S(2)}, u32[]{:S(2)}) async-start(bf16[16,24,768]{2,1,0:T(8,128)(2,1)} %broadcast_in_dim.2), calls=%async_computation.3 | async-start | bytes 1179648 | tf_op jit(solution)/shard_map/all_to_all | solution.py:293
  96.9 5.2 %add_convert_fusion = bf16[512,768]{1,0:T(8,128)(2,1)} fusion(bf16[512,768]{1,0:T(8,128)(2,1)S(1)} %collective-permute-done.1, bf16[768,2048]{1,0:T(8,128)(2,1)} %get-tuple-element.13.query_hbm, bf16[1024,2048]{1,0:T(8,128)(2,1)} %get-tuple-element.19), kind=kOutput, calls=%fused_computation.5 | convolution fusion | flops 1611792384 | bytes 6815744 | tf_op jit(solution)/shard_map/dot_general | solution.py:276
  102.2 4.0 %all-to-all-done.3 = bf16[16,24,768]{2,1,0:T(8,128)(2,1)S(1)} async-done(((bf16[16,24,768]{2,1,0:T(8,128)(2,1)}), bf16[16,24,768]{2,1,0:T(8,128)(2,1)S(1)}, u32[]{:S(2)}, u32[]{:S(2)}) %all-to-all-start.3) | async-done | bytes 589856 | tf_op jit(solution)/shard_map/all_to_all | solution.py:293
  106.1 4.9 %all-to-all-start.1 = ((bf16[8,64,768]{2,1,0:T(8,128)(2,1)}), bf16[8,64,768]{2,1,0:T(8,128)(2,1)S(1)}, u32[]{:S(2)}, u32[]{:S(2)}) async-start(bf16[8,64,768]{2,1,0:T(8,128)(2,1)} %bitcast.5), calls=%async_computation.1 | async-start | bytes 1572864 | tf_op jit(solution)/shard_map/all_to_all | solution.py:280
  111.3 10.3 %all-to-all-done.1 = bf16[8,64,768]{2,1,0:T(8,128)(2,1)S(1)} async-done(((bf16[8,64,768]{2,1,0:T(8,128)(2,1)}), bf16[8,64,768]{2,1,0:T(8,128)(2,1)S(1)}, u32[]{:S(2)}, u32[]{:S(2)}) %all-to-all-start.1) | async-done | bytes 786464 | tf_op jit(solution)/shard_map/all_to_all | solution.py:280
  121.6 0.2 multiply_reduce_fusion
  121.8 0.8 subtract_multiply_fusion
  122.6 0.1 broadcast_select_fusion.1
  122.7 1.6 %maximum_convert_fusion = f32[768,768]{1,0:T(8,128)} fusion(bf16[384,768]{1,0:T(8,128)(2,1)S(1)} %get-tuple-element.28, bf16[384,768]{1,0:T(8,128)(2,1)S(1)} %get-tuple-element.27), kind=kLoop, calls=%fused_computation.7 | loop fusion | flops 2359296 | bytes 3538944 | tf_op jit(solution)/shard_map/convert_element_type | solution.py:297
  (31 shorter events, 0.8 us)
Async XLA Ops:
  23.3 10.2 %collective-permute-start = (bf16[512,768]{1,0:T(8,128)(2,1)S(1)}, bf16[512,768]{1,0:T(8,128)(2,1)S(1)}, u32[]{:S(2)}, u32[]{:S(2)}) collective-permute-start(bf16[512,768]{1,0:T(8,128)(2,1)S(1)} %bitcast.12), channel_id=1, source_target_pairs={{0,1},{1,0},{2,3},{3,2},{4,5},{5,4},{6,7},{7,6},{8,9},{9,8},{10,11... | collective-permute-start | bytes 2359304 | tf_op jit(solution)/shard_map/ppermute | solution.py:33
  25.3 8.2 %copy-start = (f32[1024,1]{1,0:T(8,128)S(1)}, f32[1024,1]{1,0:T(8,128)}, u32[]{:S(2)}) copy-start(f32[1024,1]{1,0:T(8,128)} %copy.8.labels) | copy-start | bytes 12292
  25.3 8.2 %copy-start.1 = (s32[2048]{0:T(1024)S(1)}, s32[2048]{0:T(1024)}, u32[]{:S(2)}) copy-start(s32[2048]{0:T(1024)} %param.9) | copy-start | bytes 24580
  33.5 1.9 %copy-start.2 = (bf16[768,2048]{1,0:T(8,128)(2,1)S(1)}, bf16[768,2048]{1,0:T(8,128)(2,1)}, u32[]{:S(2)}) copy-start(bf16[768,2048]{1,0:T(8,128)(2,1)} %get-tuple-element.13.query_hbm) | copy-start | bytes 9437188
  35.4 1.9 %copy-start.3 = (bf16[768,2048]{1,0:T(8,128)(2,1)S(1)}, bf16[768,2048]{1,0:T(8,128)(2,1)}, u32[]{:S(2)}) copy-start(bf16[768,2048]{1,0:T(8,128)(2,1)} %get-tuple-element.14.states_hbm) | copy-start | bytes 9437188
  37.3 0.7 copy-start.4
  38.0 0.7 copy-start.5
  53.1 2.2 %collective-permute-start.2 = (bf16[384,768]{1,0:T(8,128)(2,1)S(1)}, bf16[384,768]{1,0:T(8,128)(2,1)S(1)}, u32[]{:S(2)}, u32[]{:S(2)}) collective-permute-start(bf16[384,768]{1,0:T(8,128)(2,1)S(1)} %get-tuple-element.22), channel_id=1, source_target_pairs={{0,1},{1,0},{2,3},{3,2},{4,5},{5,4},{6,7},{7,6},{8,9},{9,8},{10,11... | collective-permute-start | bytes 1769480 | tf_op jit(solution)/shard_map/ppermute | solution.py:33
  56.3 16.3 %all-to-all-start.2 = ((bf16[16,24,768]{2,1,0:T(8,128)(2,1)}), bf16[16,24,768]{2,1,0:T(8,128)(2,1)S(1)}, u32[]{:S(2)}, u32[]{:S(2)}) async-start(bf16[16,24,768]{2,1,0:T(8,128)(2,1)} %bitcast.6), calls=%async_computation.2 | async-start | bytes 1179648 | tf_op jit(solution)/shard_map/all_to_all | solution.py:272
  66.0 30.9 %collective-permute-start.1 = (bf16[512,768]{1,0:T(8,128)(2,1)}, bf16[512,768]{1,0:T(8,128)(2,1)S(1)}, u32[]{:S(2)}, u32[]{:S(2)}) collective-permute-start(bf16[512,768]{1,0:T(8,128)(2,1)} %fusion.6), channel_id=1, source_target_pairs={{0,1},{1,0},{2,3},{3,2},{4,5},{5,4},{6,7},{7,6},{8,9},{9,8},{10,11... | collective-permute-start | bytes 2359304 | tf_op jit(solution)/shard_map/ppermute | solution.py:33
  72.7 4.0 %collective-permute-start.3 = (bf16[24,768]{1,0:T(8,128)(2,1)S(1)}, bf16[24,768]{1,0:T(8,128)(2,1)S(1)}, u32[]{:S(2)}, u32[]{:S(2)}) collective-permute-start(bf16[24,768]{1,0:T(8,128)(2,1)S(1)} %reduce_sum.32), channel_id=1, source_target_pairs={{0,32},{1,33},{2,34},{3,35},{4,36},{5,37},{6,38},{7,39},{8,40},{9,... | collective-permute-start | bytes 110600 | tf_op jit(solution)/shard_map/ppermute | solution.py:33
  76.7 10.2 %collective-permute-start.6 = (bf16[24,768]{1,0:T(8,128)(2,1)S(1)}, bf16[24,768]{1,0:T(8,128)(2,1)S(1)}, u32[]{:S(2)}, u32[]{:S(2)}) collective-permute-start(bf16[24,768]{1,0:T(8,128)(2,1)S(1)} %add_convert_fusion.3), channel_id=1, source_target_pairs={{0,192},{1,193},{2,194},{3,195},{4,196},{5,197},{6,198},{7,199},{8... | collective-permute-start | bytes 110600 | tf_op jit(solution)/shard_map/ppermute | solution.py:33
  83.1 6.1 %collective-permute-start.5 = (bf16[24,768]{1,0:T(8,128)(2,1)S(1)}, bf16[24,768]{1,0:T(8,128)(2,1)S(1)}, u32[]{:S(2)}, u32[]{:S(2)}) collective-permute-start(bf16[24,768]{1,0:T(8,128)(2,1)S(1)} %add_convert_fusion.3), channel_id=1, source_target_pairs={{0,64},{1,65},{2,66},{3,67},{4,68},{5,69},{6,70},{7,71},{8,72},{9,... | collective-permute-start | bytes 110600 | tf_op jit(solution)/shard_map/ppermute | solution.py:33
  83.1 8.1 %collective-permute-start.4 = (bf16[24,768]{1,0:T(8,128)(2,1)S(1)}, bf16[24,768]{1,0:T(8,128)(2,1)S(1)}, u32[]{:S(2)}, u32[]{:S(2)}) collective-permute-start(bf16[24,768]{1,0:T(8,128)(2,1)S(1)} %add_convert_fusion.3), channel_id=1, source_target_pairs={{0,128},{1,129},{2,130},{3,131},{4,132},{5,133},{6,134},{7,135},{8... | collective-permute-start | bytes 110600 | tf_op jit(solution)/shard_map/ppermute | solution.py:33
  92.1 14.0 %all-to-all-start.3 = ((bf16[16,24,768]{2,1,0:T(8,128)(2,1)}), bf16[16,24,768]{2,1,0:T(8,128)(2,1)S(1)}, u32[]{:S(2)}, u32[]{:S(2)}) async-start(bf16[16,24,768]{2,1,0:T(8,128)(2,1)} %broadcast_in_dim.2), calls=%async_computation.3 | async-start | bytes 1179648 | tf_op jit(solution)/shard_map/all_to_all | solution.py:293
  96.9 14.1 %copy-start.7 = (f32[64,1]{1,0:T(8,128)S(1)}, f32[64,1]{1,0:T(8,128)}, u32[]{:S(2)}) copy-start(f32[64,1]{1,0:T(8,128)} %get-tuple-element.20) | copy-start | bytes 772
  102.2 19.4 %copy-start.6 = (bf16[64,768]{1,0:T(8,128)(2,1)S(1)}, bf16[64,768]{1,0:T(8,128)(2,1)}, u32[]{:S(2)}) copy-start(bf16[64,768]{1,0:T(8,128)(2,1)} %attempts.1) | copy-start | bytes 294916
  106.1 15.4 %all-to-all-start.1 = ((bf16[8,64,768]{2,1,0:T(8,128)(2,1)}), bf16[8,64,768]{2,1,0:T(8,128)(2,1)S(1)}, u32[]{:S(2)}, u32[]{:S(2)}) async-start(bf16[8,64,768]{2,1,0:T(8,128)(2,1)} %bitcast.5), calls=%async_computation.1 | async-start | bytes 1572864 | tf_op jit(solution)/shard_map/all_to_all | solution.py:280
  111.2 11.5 %collective-permute-start.7 = (bf16[384,768]{1,0:T(8,128)(2,1)S(1)}, bf16[384,768]{1,0:T(8,128)(2,1)S(1)}, u32[]{:S(2)}, u32[]{:S(2)}) collective-permute-start(bf16[384,768]{1,0:T(8,128)(2,1)S(1)} %bitcast.16), channel_id=1, source_target_pairs={{0,1},{1,0},{2,3},{3,2},{4,5},{5,4},{6,7},{7,6},{8,9},{9,8},{10,11... | collective-permute-start | bytes 1769480 | tf_op jit(solution)/shard_map/ppermute | solution.py:33
